TPU v7x, 32 devices: a whole 2x2x4 slice. The times are simulated.
32 devices in a mesh: band: 4 (over z), sector: 8 (over y, x, core).
Axes of the slice: x: 2, y: 2, z: 4, core: 2. Of those that a mesh axis runs over, the one named last changes fastest.
Arguments:
- node_states: bfloat16 [16, 128, 512], P('band', 'sector'), may hold values from -6 to 6
- edge_states: bfloat16 [32, 512, 512], P(('band', 'sector')), may hold values from -6 to 6
- senders: int32 [32, 512], P(('band', 'sector')), may hold values from 0 to 351, as said below
- receivers: int32 [32, 512], P(('band', 'sector')), may hold values from 0 to 63
- edge_count: int32 [32], P(('band', 'sector')), may hold values from 128 to 512, as said below
- edge_hidden: bfloat16 [2, 1536, 512], replicated, may hold values from -0.15625 to 0.15625
- edge_offset: float32 [2, 512], replicated, may hold values from -3 to 3
- edge_output: bfloat16 [2, 512, 512], replicated, may hold values from -0.25 to 0.25
- edge_scale: float32 [2, 512], replicated, may hold values from 0.5 to 1.5
- node_hidden: bfloat16 [2, 1024, 512], replicated, may hold values from -0.1875 to 0.1875
- node_offset: float32 [2, 512], replicated, may hold values from -3 to 3
- node_output: bfloat16 [2, 512, 512], replicated, may hold values from -0.25 to 0.25
- node_scale: float32 [2, 512], replicated, may hold values from 0.5 to 1.5
- output_cotangent: bfloat16 [16, 128, 512], P('band', 'sector'), may hold values from -6 to 6
Outputs:
- node_result: bfloat16 [16, 128, 512], P('band', 'sector')
- node_gradient: float32 [16, 128, 512], P('band', 'sector')
- edge_gradient: float32 [32, 512, 512], P(('band', 'sector'))
- edge_hidden_gradient: float32 [2, 1536, 512], replicated
- edge_offset_gradient: float32 [2, 512], replicated
- edge_output_gradient: float32 [2, 512, 512], replicated
- edge_scale_gradient: float32 [2, 512], replicated
- node_hidden_gradient: float32 [2, 1024, 512], replicated
- node_offset_gradient: float32 [2, 512], replicated
- node_output_gradient: float32 [2, 512, 512], replicated
- node_scale_gradient: float32 [2, 512], replicated
Inputs may be any that keep to these rules, and one draw needn't show every extreme that they name: `senders`: an entry below 288 names a cell of the device's extended block (row-major, 12 rows); devices of the first band never name its first 4 rows, devices of the last band never its last 4 rows. An entry 288 + c names coarse node c. `edge_count`: slots at or past a device's count hold no edge. Some device has all 512 slots live.
All inputs are finite; a program needn't handle non-finite values.
Results may differ from a plain program's by a relative error of at most 0.019.
Values may be sent and summed in bfloat16 or wider, within the bound.
No kernel may reach another device: no remote copies, remote signals or barrier semaphores. Data moves between devices by JAX's collectives and lax.ppermute only.
A program may use at most 128 MiB of HBM per device.

v0:
```python
import math
import jax
import jax.numpy as jnp
from jax import lax
from jax.sharding import PartitionSpec as P

CO = 2
epsilon = 1e-05


def shifted(shard, axis, by):
    length = lax.axis_size(axis)
    return lax.ppermute(shard, axis, [(i, (i + by) % length) for i in range(length)])


def passed_along(block, axis, distance):
    devices = range(lax.axis_size(axis))
    route = [(i - distance, i) for i in devices if i - distance in devices]
    return lax.ppermute(block, axis, route)


def extended_2(cells, sides, width):
    for axis, dim in sides:
        count = lax.axis_size(axis)
        head = lax.slice_in_dim(cells, 0, width, axis=dim)
        tail = lax.slice_in_dim(cells, cells.shape[dim] - width, cells.shape[dim], axis=dim)
        cells = jnp.concatenate(
            [
                lax.ppermute(tail, axis, [(i, (i + 1) % count) for i in range(count)]),
                cells,
                lax.ppermute(head, axis, [((i + 1) % count, i) for i in range(count)]),
            ],
            axis=dim,
        )
    return cells


def mlp_forward(inputs, first_weight, first_bias, second_weight, norm_gain):
    pre_act = jnp.dot(inputs, first_weight, preferred_element_type=jnp.float32) + first_bias
    sigmoid_val = jax.nn.sigmoid(pre_act)
    activated = (pre_act * sigmoid_val).astype(jnp.bfloat16)
    mixed = jnp.dot(activated, second_weight, preferred_element_type=jnp.float32)
    centered = mixed - jnp.mean(mixed, axis=-1, keepdims=True)
    inv_std = lax.rsqrt(jnp.mean(centered * centered, axis=-1, keepdims=True) + epsilon)
    normed = centered * inv_std
    return (normed * norm_gain, (inputs, pre_act, sigmoid_val, activated, normed, inv_std))


def mlp_backward(grad_out, saved, first_weight, second_weight, norm_gain):
    inputs, pre_act, sigmoid_val, activated, normed, inv_std = saved
    grad_gain = jnp.sum(grad_out * normed, axis=0)
    grad_normed = grad_out * norm_gain
    grad_mixed = inv_std * (
        grad_normed
        - jnp.mean(grad_normed, axis=-1, keepdims=True)
        - normed * jnp.mean(grad_normed * normed, axis=-1, keepdims=True)
    )
    mixed_low = grad_mixed.astype(jnp.bfloat16)
    grad_second = lax.dot_general(
        activated, mixed_low, (((0,), (0,)), ((), ())), preferred_element_type=jnp.float32
    )
    grad_act = lax.dot_general(
        mixed_low, second_weight, (((1,), (1,)), ((), ())), preferred_element_type=jnp.float32
    )
    grad_pre = grad_act * sigmoid_val * (1.0 + pre_act * (1.0 - sigmoid_val))
    grad_bias = jnp.sum(grad_pre, axis=0)
    pre_low = grad_pre.astype(jnp.bfloat16)
    grad_first = lax.dot_general(
        inputs, pre_low, (((0,), (0,)), ((), ())), preferred_element_type=jnp.float32
    )
    grad_inputs = lax.dot_general(
        pre_low, first_weight, (((1,), (1,)), ((), ())), preferred_element_type=jnp.float32
    )
    return (grad_inputs, (grad_first, grad_bias, grad_second, grad_gain))


def fold_sector(grad_block, reach):
    kept = grad_block.shape[1] - 2 * reach
    middle = grad_block[:, reach : reach + kept]
    from_next = shifted(grad_block[:, :reach].astype(jnp.bfloat16), "sector", -1).astype(
        jnp.float32
    )
    from_prev = shifted(grad_block[:, reach + kept :].astype(jnp.bfloat16), "sector", 1).astype(
        jnp.float32
    )
    return middle.at[:, kept - reach :].add(from_next).at[:, :reach].add(from_prev)


def fold_band(grad_block, reach):
    kept = grad_block.shape[0] - 2 * reach
    middle = grad_block[reach : reach + kept]
    from_next = passed_along(grad_block[:reach].astype(jnp.bfloat16), "band", -1).astype(
        jnp.float32
    )
    from_prev = passed_along(grad_block[reach + kept :].astype(jnp.bfloat16), "band", 1).astype(
        jnp.float32
    )
    return middle.at[kept - reach :].add(from_next).at[:reach].add(from_prev)


def local(
    node_states,
    edge_states,
    senders,
    receivers,
    edge_count,
    edge_hidden,
    edge_offset,
    edge_output,
    edge_scale,
    node_hidden,
    node_offset,
    node_output,
    node_scale,
    output_cotangent,
):
    lat_rows, lon_cols, width = node_states.shape
    node_rows = lat_rows * lon_cols
    slots = edge_states.shape[1]
    depth = edge_hidden.shape[0]
    ext_rows = 3 * lat_rows * (lon_cols + 2 * lat_rows)
    table_rows = ext_rows + CO * lax.axis_size("band") * lax.axis_size("sector")
    edge_rows = edge_states[0]
    send_index = senders[0]
    recv_index = receivers[0]
    live_count = edge_count[0]
    live_mask = (jnp.arange(slots, dtype=jnp.int32) < live_count).astype(jnp.float32)[:, None]
    incidence = (recv_index[:, None] == jnp.arange(node_rows, dtype=jnp.int32)[None, :]).astype(
        jnp.float32
    )
    sender_onehot = (
        send_index[:, None] == jnp.arange(table_rows, dtype=jnp.int32)[None, :]
    ).astype(jnp.float32)
    state = node_states.reshape(node_rows, width)
    records = []
    for depth_index in range(depth):
        edge_params = (
            edge_hidden[depth_index],
            edge_offset[depth_index],
            edge_output[depth_index],
            edge_scale[depth_index],
        )
        node_params = (
            node_hidden[depth_index],
            node_offset[depth_index],
            node_output[depth_index],
            node_scale[depth_index],
        )
        extended = extended_2(
            state.reshape(lat_rows, lon_cols, width), (("band", 0), ("sector", 1)), lat_rows
        )
        coarse = lax.all_gather(state[:CO], ("band", "sector"), axis=0, tiled=True)
        table = jnp.concatenate([extended.reshape(ext_rows, width), coarse], axis=0)
        inputs = jnp.concatenate(
            [edge_rows, jnp.take(table, send_index, axis=0), jnp.take(state, recv_index, axis=0)],
            axis=1,
        )
        result, edge_saved = mlp_forward(
            inputs, edge_params[0], edge_params[1], edge_params[2], edge_params[3]
        )
        update = result * live_mask
        summed = lax.dot_general(
            incidence,
            update,
            (((0,), (0,)), ((), ())),
            precision=lax.Precision.HIGHEST,
            preferred_element_type=jnp.float32,
        )
        node_inputs = jnp.concatenate([state, summed.astype(jnp.bfloat16)], axis=1)
        node_delta, node_saved = mlp_forward(
            node_inputs, node_params[0], node_params[1], node_params[2], node_params[3]
        )
        records.append((inputs, edge_saved, node_saved))
        edge_rows = (edge_rows.astype(jnp.float32) + update).astype(jnp.bfloat16)
        state = (state.astype(jnp.float32) + node_delta).astype(jnp.bfloat16)
    node_result = state.reshape(lat_rows, lon_cols, width)
    grad_state = output_cotangent.reshape(node_rows, width).astype(jnp.float32)
    grad_edges = jnp.zeros((slots, width), jnp.float32)
    per_layer = [None] * depth
    for depth_index in reversed(range(depth)):
        inputs, edge_saved, node_saved = records[depth_index]
        edge_params = (
            edge_hidden[depth_index],
            edge_offset[depth_index],
            edge_output[depth_index],
            edge_scale[depth_index],
        )
        grad_in, node_grads = mlp_backward(
            grad_state,
            node_saved,
            node_hidden[depth_index],
            node_output[depth_index],
            node_scale[depth_index],
        )
        grad_state = grad_state + grad_in[:, :width]
        spread = jnp.dot(
            incidence,
            grad_in[:, width:],
            precision=lax.Precision.HIGHEST,
            preferred_element_type=jnp.float32,
        )
        flow_grad = (spread + grad_edges) * live_mask
        grad_inputs, edge_grads = mlp_backward(
            flow_grad, edge_saved, edge_params[0], edge_params[2], edge_params[3]
        )
        grad_edges = grad_edges + grad_inputs[:, :width]
        grad_state = grad_state + lax.dot_general(
            incidence,
            grad_inputs[:, 2 * width :],
            (((0,), (0,)), ((), ())),
            precision=lax.Precision.HIGHEST,
            preferred_element_type=jnp.float32,
        )
        table_grad = lax.dot_general(
            sender_onehot,
            grad_inputs[:, width : 2 * width],
            (((0,), (0,)), ((), ())),
            precision=lax.Precision.HIGHEST,
            preferred_element_type=jnp.float32,
        )
        ext_grad = table_grad[:ext_rows].reshape(3 * lat_rows, lon_cols + 2 * lat_rows, width)
        coarse_grad = table_grad[ext_rows:]
        returned = fold_band(fold_sector(ext_grad, lat_rows), lat_rows)
        grad_state = grad_state + returned.reshape(node_rows, width)
        layer_grads = edge_grads + node_grads
        summed_grads = lax.psum(
            (
                layer_grads[0],
                layer_grads[1],
                layer_grads[2],
                layer_grads[3],
                layer_grads[4],
                layer_grads[5],
                layer_grads[6],
                layer_grads[7],
                coarse_grad,
            ),
            ("band", "sector"),
        )
        own_coarse = lax.dynamic_slice_in_dim(
            summed_grads[8], lax.axis_index(("band", "sector")) * CO, CO, 0
        )
        per_layer[depth_index] = tuple(summed_grads[:8])
        grad_state = grad_state.at[:CO].add(own_coarse)
    stacked = [
        jnp.stack([per_layer[depth_index][item] for depth_index in range(depth)])
        for item in range(8)
    ]
    factor = 1.0 / math.sqrt(node_rows * lax.axis_size("band") * lax.axis_size("sector"))
    return (
        node_result,
        grad_state.reshape(lat_rows, lon_cols, width),
        grad_edges[None],
        stacked[0] * factor,
        stacked[1] * factor,
        stacked[2] * factor,
        stacked[3] * factor,
        stacked[4] * factor,
        stacked[5] * factor,
        stacked[6] * factor,
        stacked[7] * factor,
    )


def solution(mesh):
    return jax.shard_map(
        local,
        mesh=mesh,
        in_specs=(
            P("band", "sector", None),
            P(("band", "sector"), None, None),
            P(("band", "sector"), None),
            P(("band", "sector"), None),
            P(("band", "sector")),
            P(),
            P(),
            P(),
            P(),
            P(),
            P(),
            P(),
            P(),
            P("band", "sector", None),
        ),
        out_specs=(
            P("band", "sector", None),
            P("band", "sector", None),
            P(("band", "sector"), None, None),
            P(),
            P(),
            P(),
            P(),
            P(),
            P(),
            P(),
            P(),
        ),
        check_vma=False,
    )
```

profile of v0, /device:TPU:0, one launch (start us, length us, event | category | flops | bytes accessed | tf_op | source)
XLA Modules:
  0.0 573.9 jit_solution(11229786818335599624)
XLA Ops:
  7.3 3.1 collective-permute-start
  10.4 2.1 collective-permute-start.1
  15.3 2.9 gather_fusion.1
  22.3 39.2 %all-gather = bf16[32,2,512]{2,1,0:T(2,128)(2,1)S(1)} all-gather(bf16[1,2,512]{2,1,0:T(2,128)(2,1)S(1)} %slice_bitcast_fusion.1), channel_id=1, replica_groups=mesh['band'=4,'sector'=8] {'band','sector'}, dimensions={0}, use_global_device_ids=true | all-gather | bytes 67584 | tf_op jit(solution)/shard_map/all_gather | solution.py:152
  62.5 2.0 gather_fusion
  64.8 2.6 fusion.15
  70.5 2.0 gather_fusion.3
  72.6 2.0 collective-permute-start.4
  79.4 37.3 %all-gather.1 = bf16[32,2,512]{2,1,0:T(2,128)(2,1)S(1)} all-gather(bf16[1,2,512]{2,1,0:T(2,128)(2,1)S(1)} %slice_bitcast_fusion), channel_id=1, replica_groups=mesh['band'=4,'sector'=8] {'band','sector'}, dimensions={0}, use_global_device_ids=true | all-gather | bytes 67584 | tf_op jit(solution)/shard_map/all_gather | solution.py:152
  119.2 2.7 fusion.18
  132.9 2.7 convolution_bitcast_fusion
  145.1 3.2 collective-permute-done.9
  153.8 2.9 collective-permute-done.10
  158.5 109.4 %all-reduce.5.cloned.1.call-done = f32[64,512]{1,0:T(8,128)} async-done(((f32[64,512]{1,0:T(8,128)}), f32[64,512]{1,0:T(8,128)}) %all-reduce.5.cloned.1.call-update) | async-done | bytes 131088 | tf_op jit(solution)/shard_map/psum | solution.py:226
  277.2 2.7 convolution_bitcast_fusion.1
  290.1 2.5 copy.42
  292.6 42.0 %all-reduce = (f32[1,512]{1,0:T(1,128)S(1)}, f32[1,512]{1,0:T(1,128)S(1)}, f32[1,512]{1,0:T(1,128)S(1)}, f32[1,512]{1,0:T(1,128)S(1)}, f32[1,512]{1,0:T(1,128)S(...) all-reduce(f32[1,512]{1,0:T(1,128)S(1)} %bitcast.197, ...), channel_id=1, replica_groups=mesh['band'=4,'sector'=8] {'band','sector'}, use_global_device_ids=true, to_apply=%region_23.26 | all-reduce | flops 4096 | bytes 32768 | tf_op jit(solution)/shard_map/psum | solution.py:226
  335.8 2.8 add_bitcast_fusion
  340.1 2.5 copy.40
  346.9 2.5 collective-permute-start.15
  353.0 4.3 collective-permute-done.14
  359.7 193.0 %all-reduce.7.cloned.1.call-done = (f32[64,512]{1,0:T(8,128)}, f32[1,1536,512]{2,1,0:T(8,128)}, f32[1,1536,512]{2,1,0:T(8,128)}, f32[1,512,512]{2,1,0:T(8,128)},...) async-done(((f32[64,512]{1,0:T(8,128)}, f32[1,1536,512]{2,1,0:T(8,128)}, ...) | async-done | bytes 14811152 | tf_op jit(solution)/shard_map/psum | solution.py:226
  553.5 6.5 %maximum_multiply_fusion = f32[2,1536,512]{2,1,0:T(8,128)} fusion(f32[1,1536,512]{2,1,0:T(8,128)} %get-tuple-element.207, f32[1,1536,512]{2,1,0:T(8,128)} %get-tuple-element.208), kind=kLoop, calls=%fused_computation.4 | loop fusion | flops 3145728 | bytes 12582912 | tf_op jit(solution)/shard_map/mul | solution.py:254
  563.0 2.5 maximum_multiply_fusion.1
  (280 shorter events, 82.6 us)
Async XLA Ops:
  7.2 260.8 %all-reduce.5.cloned.1.call-start = ((), (), s32[]{:S(2)}) async-start(), calls=%async_computation | async-start | bytes 262144 | tf_op jit(solution)/shard_map/psum | solution.py:226
  7.3 13.2 %collective-permute-start = (bf16[4,16,512]{2,1,0:T(8,128)(2,1)}, bf16[4,16,512]{2,1,0:T(8,128)(2,1)S(1)}, u32[]{:S(2)}, u32[]{:S(2)}) collective-permute-start(bf16[4,16,512]{2,1,0:T(8,128)(2,1)} %param.46), channel_id=1, source_target_pairs={{0,8},{8,16},{16,24},{24,0},{1,9},{9,17},{17,25},{25,1},{2,10},{10... | collective-permute-start | bytes 196616 | tf_op jit(solution)/shard_map/ppermute | solution.py:29
  10.4 10.1 %collective-permute-start.1 = (bf16[4,16,512]{2,1,0:T(8,128)(2,1)}, bf16[4,16,512]{2,1,0:T(8,128)(2,1)S(1)}, u32[]{:S(2)}, u32[]{:S(2)}) collective-permute-start(bf16[4,16,512]{2,1,0:T(8,128)(2,1)} %param.46), channel_id=1, source_target_pairs={{8,0},{16,8},{24,16},{0,24},{9,1},{17,9},{25,17},{1,25},{10,2},{18... | collective-permute-start | bytes 196616 | tf_op jit(solution)/shard_map/ppermute | solution.py:31
  19.7 54.9 %copy-start.35 = (f32[1,512]{1,0:T(1,128)}, f32[1,512]{1,0:T(1,128)S(1)}, u32[]{:S(2)}) copy-start(f32[1,512]{1,0:T(1,128)S(1)} %get-tuple-element.234) | copy-start | bytes 6148
  20.6 41.8 %collective-permute-start.3 = (bf16[12,4,512]{2,1,0:T(4,128)(2,1)S(1)}, bf16[12,4,512]{2,1,0:T(4,128)(2,1)S(1)}, u32[]{:S(2)}, u32[]{:S(2)}) collective-permute-start(bf16[12,4,512]{2,1,0:T(4,128)(2,1)S(1)} %get-tuple-element.226), channel_id=1, source_target_pairs={{1,0},{2,1},{3,2},{4,3},{5,4},{6,5},{7,6},{0,7},{9,8},{10,9},{11,1... | collective-permute-start | bytes 147464 | tf_op jit(solution)/shard_map/ppermute | solution.py:31
  22.2 40.1 %collective-permute-start.2 = (bf16[12,4,512]{2,1,0:T(4,128)(2,1)S(1)}, bf16[12,4,512]{2,1,0:T(4,128)(2,1)S(1)}, u32[]{:S(2)}, u32[]{:S(2)}) collective-permute-start(bf16[12,4,512]{2,1,0:T(4,128)(2,1)S(1)} %get-tuple-element.225), channel_id=1, source_target_pairs={{0,1},{1,2},{2,3},{3,4},{4,5},{5,6},{6,7},{7,0},{8,9},{9,10},{10,1... | collective-permute-start | bytes 147464 | tf_op jit(solution)/shard_map/ppermute | solution.py:29
  72.5 4.4 collective-permute-start.5
  72.6 6.2 %collective-permute-start.4 = (bf16[4,16,512]{2,1,0:T(8,128)(2,1)S(1)}, bf16[4,16,512]{2,1,0:T(8,128)(2,1)S(1)}, u32[]{:S(2)}, u32[]{:S(2)}) collective-permute-start(bf16[4,16,512]{2,1,0:T(8,128)(2,1)S(1)} %bitcast.142), channel_id=1, source_target_pairs={{0,8},{8,16},{16,24},{24,0},{1,9},{9,17},{17,25},{25,1},{2,10},{10... | collective-permute-start | bytes 196616 | tf_op jit(solution)/shard_map/ppermute | solution.py:29
  78.8 37.9 %collective-permute-start.7 = (bf16[12,4,512]{2,1,0:T(4,128)(2,1)S(1)}, bf16[12,4,512]{2,1,0:T(4,128)(2,1)S(1)}, u32[]{:S(2)}, u32[]{:S(2)}) collective-permute-start(bf16[12,4,512]{2,1,0:T(4,128)(2,1)S(1)} %get-tuple-element.224), channel_id=1, source_target_pairs={{1,0},{2,1},{3,2},{4,3},{5,4},{6,5},{7,6},{0,7},{9,8},{10,9},{11,1... | collective-permute-start | bytes 147464 | tf_op jit(solution)/shard_map/ppermute | solution.py:31
  78.9 37.9 %collective-permute-start.6 = (bf16[12,4,512]{2,1,0:T(4,128)(2,1)S(1)}, bf16[12,4,512]{2,1,0:T(4,128)(2,1)S(1)}, u32[]{:S(2)}, u32[]{:S(2)}) collective-permute-start(bf16[12,4,512]{2,1,0:T(4,128)(2,1)S(1)} %get-tuple-element.223), channel_id=1, source_target_pairs={{0,1},{1,2},{2,3},{3,4},{4,5},{5,6},{6,7},{7,0},{8,9},{9,10},{10,1... | collective-permute-start | bytes 147464 | tf_op jit(solution)/shard_map/ppermute | solution.py:29
  138.9 5.3 collective-permute-start.8
  143.5 129.1 %copy-start.2 = (f32[512,512]{0,1:T(8,128)}, f32[512,512]{0,1:T(8,128)S(1)}, u32[]{:S(2)}) copy-start(f32[512,512]{0,1:T(8,128)S(1)} %copy.41) | copy-start | bytes 3145732
  143.5 4.8 collective-permute-start.9
  144.1 408.6 %all-reduce.7.cloned.1.call-start = ((), (), s32[]{:S(2)}) async-start(), calls=%async_computation.1 | async-start | bytes 29622272 | tf_op jit(solution)/shard_map/psum | solution.py:226
  145.1 124.5 %copy-start.30 = (f32[64,512]{1,0:T(8,128)S(1)}, f32[64,512]{1,0:T(8,128)}, u32[]{:S(2)}) copy-start(f32[64,512]{1,0:T(8,128)} %copy-done.29) | copy-start | bytes 393220
  149.2 4.6 collective-permute-start.11
  150.5 6.2 %collective-permute-start.10 = (bf16[4,16,512]{2,1,0:T(8,128)(2,1)S(1)}, bf16[4,16,512]{2,1,0:T(8,128)(2,1)S(1)}, u32[]{:S(2)}, u32[]{:S(2)}) collective-permute-start(bf16[4,16,512]{2,1,0:T(8,128)(2,1)S(1)} %get-tuple-element.221), channel_id=1, source_target_pairs={{8,0},{16,8},{24,16},{9,1},{17,9},{25,17},{10,2},{18,10},{26,18},{... | collective-permute-start | bytes 196616 | tf_op jit(solution)/shard_map/ppermute | solution.py:19
  153.8 118.8 %copy-start.36 = (f32[1,512]{1,0:T(1,128)S(1)}, f32[1,512]{1,0:T(1,128)}, u32[]{:S(2)}) copy-start(f32[1,512]{1,0:T(1,128)} %copy-done.35) | copy-start | bytes 6148
  153.8 118.8 %copy-start.38 = (f32[512]{0:T(512)S(1)}, f32[512]{0:T(512)}, u32[]{:S(2)}) copy-start(f32[512]{0:T(512)} %copy-done.37) | copy-start | bytes 6148
  153.8 118.9 %copy-start.42 = (f32[512]{0:T(512)S(1)}, f32[512]{0:T(512)}, u32[]{:S(2)}) copy-start(f32[512]{0:T(512)} %copy-done.40) | copy-start | bytes 6148
  289.5 53.1 %collective-permute-start.12 = (bf16[12,4,512]{2,1,0:T(4,128)(2,1)S(1)}, bf16[12,4,512]{2,1,0:T(4,128)(2,1)S(1)}, u32[]{:S(2)}, u32[]{:S(2)}) collective-permute-start(bf16[12,4,512]{2,1,0:T(4,128)(2,1)S(1)} %get-tuple-element.216), channel_id=1, source_target_pairs={{0,7},{1,0},{2,1},{3,2},{4,3},{5,4},{6,5},{7,6},{8,15},{9,8},{10,9... | collective-permute-start | bytes 147464 | tf_op jit(solution)/shard_map/ppermute | solution.py:13
  289.7 54.5 %collective-permute-start.13 = (bf16[12,4,512]{2,1,0:T(4,128)(2,1)S(1)}, bf16[12,4,512]{2,1,0:T(4,128)(2,1)S(1)}, u32[]{:S(2)}, u32[]{:S(2)}) collective-permute-start(bf16[12,4,512]{2,1,0:T(4,128)(2,1)S(1)} %get-tuple-element.215), channel_id=1, source_target_pairs={{0,1},{1,2},{2,3},{3,4},{4,5},{5,6},{6,7},{7,0},{8,9},{9,10},{10,1... | collective-permute-start | bytes 147464 | tf_op jit(solution)/shard_map/ppermute | solution.py:13
  346.9 6.0 %collective-permute-start.15 = (bf16[4,16,512]{2,1,0:T(8,128)(2,1)S(1)}, bf16[4,16,512]{2,1,0:T(8,128)(2,1)S(1)}, u32[]{:S(2)}, u32[]{:S(2)}) collective-permute-start(bf16[4,16,512]{2,1,0:T(8,128)(2,1)S(1)} %get-tuple-element.220), channel_id=1, source_target_pairs={{0,8},{8,16},{16,24},{1,9},{9,17},{17,25},{2,10},{10,18},{18,26},{... | collective-permute-start | bytes 196616 | tf_op jit(solution)/shard_map/ppermute | solution.py:19
  349.4 7.8 %collective-permute-start.14 = (bf16[4,16,512]{2,1,0:T(8,128)(2,1)S(1)}, bf16[4,16,512]{2,1,0:T(8,128)(2,1)S(1)}, u32[]{:S(2)}, u32[]{:S(2)}) collective-permute-start(bf16[4,16,512]{2,1,0:T(8,128)(2,1)S(1)} %get-tuple-element.219), channel_id=1, source_target_pairs={{8,0},{16,8},{24,16},{9,1},{17,9},{25,17},{10,2},{18,10},{26,18},{... | collective-permute-start | bytes 196616 | tf_op jit(solution)/shard_map/ppermute | solution.py:19
  (59 other events, 374.0 us)
Sparse Core Ops, SparseCore 0:
  144.2 123.7 all-reduce.4
  287.2 265.4 all-reduce.6
where the time goes:
time: 575 us; the launch traced here: 574 us
  waiting for transfers between devices  317 us (55%)
  blocking collectives  118 us (21%)
  matrix products  40.5 us (7%)
  other arithmetic  33.4 us (6%)
  local copies, waits for them, and re-layouts  31 us (5%)
  starting transfers between devices  17.3 us (3%)
  between operations  15.9 us (3%)
    psum x2, waiting for transfers between devices, local(): lax.psum((layer_grads[0], layer_grads[1], layer_grads[2], layer_grads[3],...  302 us
    all_gather x2, blocking collectives, local(): coarse = lax.all_gather(state[:CO], ('band', 'sector'), axis=0, tiled=True)  76.5 us
    psum x1, blocking collectives, local(): lax.psum((layer_grads[0], layer_grads[1], layer_grads[2], layer_grads[3],...  42 us
    unnamed x140, local copies, waits for them, and re-layouts  13.2 us
  transfers between devices with their start and end apart: 18, of which 8 were waited for; matrix products, arithmetic and copies ran while one was open for 7% of the time, Pallas kernels for 0%

commit v1 on v0

--- a/solution.py
+++ b/solution.py
@@ -224,18 +224,21 @@
         grad_state = grad_state + returned.reshape(node_rows, width)
         layer_grads = edge_grads + node_grads
         summed_grads = lax.psum(
-            (
-                layer_grads[0],
-                layer_grads[1],
-                layer_grads[2],
-                layer_grads[3],
-                layer_grads[4],
-                layer_grads[5],
-                layer_grads[6],
-                layer_grads[7],
-                coarse_grad,
+            lax.psum(
+                (
+                    layer_grads[0],
+                    layer_grads[1],
+                    layer_grads[2],
+                    layer_grads[3],
+                    layer_grads[4],
+                    layer_grads[5],
+                    layer_grads[6],
+                    layer_grads[7],
+                    coarse_grad,
+                ),
+                "sector",
             ),
-            ("band", "sector"),
+            "band",
         )
         own_coarse = lax.dynamic_slice_in_dim(
             summed_grads[8], lax.axis_index(("band", "sector")) * CO, CO, 0

time: 575 us -> 973 us (1.69)
  waiting for transfers between devices: 317 us -> 709 us
    psum x0 -> x2, waiting for transfers between devices: none -> 456 us  [local(): lax.psum(lax.psum((layer_grads[0], layer_grads[1], layer_grads[2], layer_...]
    psum x2, waiting for transfers between devices: 302 us -> 239 us  [local(): lax.psum((layer_grads[0], layer_grads[1], layer_grads[2], layer_grads[3],...]
    psum x0 -> x1, blocking collectives: none -> 23.6 us  [local(): lax.psum(lax.psum((layer_grads[0], layer_grads[1], layer_grads[2], layer_...]
    psum x1, blocking collectives: 42 us -> 26.1 us  [local(): lax.psum((layer_grads[0], layer_grads[1], layer_grads[2], layer_grads[3],...]
  transfers between devices with their start and end apart: 18 -> 20, of which waited for: 8 -> 9; matrix products, arithmetic and copies ran while one was open for 7% -> 4% of each run, Pallas kernels for 0% -> 0%
where the time goes in v1:
time: 973 us; the launch traced here: 972 us
  waiting for transfers between devices  709 us (73%)
  blocking collectives  126 us (13%)
  matrix products  42.1 us (4%)
  other arithmetic  33.3 us (3%)
  local copies, waits for them, and re-layouts  29.2 us (3%)
  starting transfers between devices  16.8 us (2%)
  between operations  15.6 us (2%)
    psum x2, waiting for transfers between devices, local(): lax.psum(lax.psum((layer_grads[0], layer_grads[1], layer_grads[2], layer_...  456 us
    psum x2, waiting for transfers between devices, local(): lax.psum((layer_grads[0], layer_grads[1], layer_grads[2], layer_grads[3],...  239 us
    all_gather x2, blocking collectives, local(): coarse = lax.all_gather(state[:CO], ('band', 'sector'), axis=0, tiled=True)  76.5 us
    psum x1, blocking collectives, local(): lax.psum((layer_grads[0], layer_grads[1], layer_grads[2], layer_grads[3],...  26.1 us
    psum x1, blocking collectives, local(): lax.psum(lax.psum((layer_grads[0], layer_grads[1], layer_grads[2], layer_...  23.6 us
  transfers between devices with their start and end apart: 20, of which 9 were waited for; matrix products, arithmetic and copies ran while one was open for 4% of the time, Pallas kernels for 0%

profile of v1, /device:TPU:0, one launch (start us, length us, event | category | flops | bytes accessed | tf_op | source)
XLA Modules:
  0.0 972.0 jit_solution(6243084011863799762)
XLA Ops:
  7.3 3.1 collective-permute-start
  10.4 2.1 collective-permute-start.1
  15.3 2.9 gather_fusion.1
  22.3 39.2 %all-gather = bf16[32,2,512]{2,1,0:T(2,128)(2,1)S(1)} all-gather(bf16[1,2,512]{2,1,0:T(2,128)(2,1)S(1)} %slice_bitcast_fusion.1), channel_id=1, replica_groups=mesh['band'=4,'sector'=8] {'band','sector'}, dimensions={0}, use_global_device_ids=true | all-gather | bytes 67584 | tf_op jit(solution)/shard_map/all_gather | solution.py:152
  64.8 2.6 fusion.15
  72.6 2.0 collective-permute-start.4
  79.4 37.3 %all-gather.1 = bf16[32,2,512]{2,1,0:T(2,128)(2,1)S(1)} all-gather(bf16[1,2,512]{2,1,0:T(2,128)(2,1)S(1)} %slice_bitcast_fusion), channel_id=1, replica_groups=mesh['band'=4,'sector'=8] {'band','sector'}, dimensions={0}, use_global_device_ids=true | all-gather | bytes 67584 | tf_op jit(solution)/shard_map/all_gather | solution.py:152
  119.3 2.7 fusion.18
  132.9 2.7 fusion.41
  142.8 3.2 collective-permute-done.9
  149.4 2.2 fusion.117
  152.0 42.7 %all-reduce.9.cloned.1.call-done = f32[64,512]{1,0:T(8,128)} async-done(((f32[64,512]{1,0:T(8,128)}), f32[64,512]{1,0:T(8,128)}) %all-reduce.9.cloned.1.call-update) | async-done | bytes 131088 | tf_op jit(solution)/shard_map/psum | solution.py:227
  197.8 33.3 %all-reduce.11.cloned.1.call-done = f32[64,512]{1,0:T(8,128)} async-done(((f32[64,512]{1,0:T(8,128)}), f32[64,512]{1,0:T(8,128)}) %all-reduce.11.cloned.1.call-update) | async-done | bytes 131088 | tf_op jit(solution)/shard_map/psum | solution.py:226
  241.0 2.7 fusion.42
  250.9 196.4 %all-reduce.13.cloned.1.call-done = (f32[64,512]{1,0:T(8,128)}, f32[1536,512]{1,0:T(8,128)}, f32[1536,512]{1,0:T(8,128)}, f32[512,512]{1,0:T(8,128)}, f32[512,51...) async-done(((f32[64,512]{1,0:T(8,128)}, f32[1536,512]{1,0:T(8,128)}, f32[1536,512]{1,0:T(8,128)}, ...) | async-done | bytes 14811152 | tf_op jit(solution)/shard_map/psum | solution.py:227
  451.0 2.5 copy.42
  453.5 26.1 %all-reduce = (f32[512]{0:T(512)S(1)}, f32[512]{0:T(512)S(1)}, f32[512]{0:T(512)S(1)}, f32[512]{0:T(512)S(1)}, f32[512]{0:T(512)S(1)}, /*index=5*/f32[512]{0:T(512)S(1)}, f32[512]{0:T(512)S(1)}, f32[512]{0:T(512)S(1)}) all-reduce(f32[512]{0:T(512)S(1)} %copy-done.57, ...), channel_id=1, replica_groups=mesh['band'=4,'sector'=8] {'sector'}, use_global_device_ids=true, to_apply=%region_28.31 | all-reduce | flops 4096 | bytes 32768 | tf_op jit(solution)/shard_map/psum | solution.py:227
  479.6 23.6 %all-reduce.2 = (f32[1,512]{1,0:T(1,128)S(1)}, f32[1,512]{1,0:T(1,128)S(1)}, f32[1,512]{1,0:T(1,128)S(1)}, f32[1,512]{1,0:T(1,128)S(1)}, f32[1,512]{1,0:T(1,128)...) all-reduce(f32[1,512]{1,0:T(1,128)S(1)} %bitcast.192, ...), channel_id=1, replica_groups=mesh['band'=4,'sector'=8] {'band'}, use_global_device_ids=true, to_apply=%region_29.32 | all-reduce | flops 4096 | bytes 32768 | tf_op jit(solution)/shard_map/psum | solution.py:226
  504.4 2.7 add_bitcast_fusion
  508.5 2.5 copy.40
  519.9 6.2 collective-permute-done.14
  528.5 422.7 %all-reduce.15.cloned.1.call-done = (f32[64,512]{1,0:T(8,128)}, f32[1,1536,512]{2,1,0:T(8,128)}, f32[1,1536,512]{2,1,0:T(8,128)}, f32[1,512,512]{2,1,0:T(8,128)}...) async-done(((f32[64,512]{1,0:T(8,128)}, f32[1,1536,512]{2,1,0:T(8,128)}, ...) | async-done | bytes 14811152 | tf_op jit(solution)/shard_map/psum | solution.py:226
  951.9 6.5 maximum_multiply_fusion
  961.4 2.5 maximum_multiply_fusion.1
  (288 shorter events, 86.0 us)
Async XLA Ops:
  7.2 187.5 %all-reduce.9.cloned.1.call-start = ((), (), s32[]{:S(2)}) async-start(), calls=%async_computation | async-start | bytes 262144 | tf_op jit(solution)/shard_map/psum | solution.py:227
  7.3 13.2 %collective-permute-start = (bf16[4,16,512]{2,1,0:T(8,128)(2,1)}, bf16[4,16,512]{2,1,0:T(8,128)(2,1)S(1)}, u32[]{:S(2)}, u32[]{:S(2)}) collective-permute-start(bf16[4,16,512]{2,1,0:T(8,128)(2,1)} %param.46), channel_id=1, source_target_pairs={{0,8},{8,16},{16,24},{24,0},{1,9},{9,17},{17,25},{25,1},{2,10},{10... | collective-permute-start | bytes 196616 | tf_op jit(solution)/shard_map/ppermute | solution.py:29
  10.4 10.1 %collective-permute-start.1 = (bf16[4,16,512]{2,1,0:T(8,128)(2,1)}, bf16[4,16,512]{2,1,0:T(8,128)(2,1)S(1)}, u32[]{:S(2)}, u32[]{:S(2)}) collective-permute-start(bf16[4,16,512]{2,1,0:T(8,128)(2,1)} %param.46), channel_id=1, source_target_pairs={{8,0},{16,8},{24,16},{0,24},{9,1},{17,9},{25,17},{1,25},{10,2},{18... | collective-permute-start | bytes 196616 | tf_op jit(solution)/shard_map/ppermute | solution.py:31
  13.9 50.9 %copy-start.46 = (pred[512]{0:T(512)(128)(4,1)}, pred[512]{0:T(512)(128)(4,1)S(1)}, u32[]{:S(2)}) copy-start(pred[512]{0:T(512)(128)(4,1)S(1)} %get-tuple-element.273) | copy-start | bytes 1540
  15.3 46.2 %copy-start.22 = (bf16[1,512,512]{2,1,0:T(8,128)(2,1)S(1)}, bf16[1,512,512]{2,1,0:T(8,128)(2,1)}, u32[]{:S(2)}) copy-start(bf16[1,512,512]{2,1,0:T(8,128)(2,1)} %param.47) | copy-start | bytes 1572868
  20.6 41.8 %collective-permute-start.3 = (bf16[12,4,512]{2,1,0:T(4,128)(2,1)S(1)}, bf16[12,4,512]{2,1,0:T(4,128)(2,1)S(1)}, u32[]{:S(2)}, u32[]{:S(2)}) collective-permute-start(bf16[12,4,512]{2,1,0:T(4,128)(2,1)S(1)} %get-tuple-element.243), channel_id=1, source_target_pairs={{1,0},{2,1},{3,2},{4,3},{5,4},{6,5},{7,6},{0,7},{9,8},{10,9},{11,1... | collective-permute-start | bytes 147464 | tf_op jit(solution)/shard_map/ppermute | solution.py:31
  22.2 40.1 %collective-permute-start.2 = (bf16[12,4,512]{2,1,0:T(4,128)(2,1)S(1)}, bf16[12,4,512]{2,1,0:T(4,128)(2,1)S(1)}, u32[]{:S(2)}, u32[]{:S(2)}) collective-permute-start(bf16[12,4,512]{2,1,0:T(4,128)(2,1)S(1)} %get-tuple-element.242), channel_id=1, source_target_pairs={{0,1},{1,2},{2,3},{3,4},{4,5},{5,6},{6,7},{7,0},{8,9},{9,10},{10,1... | collective-permute-start | bytes 147464 | tf_op jit(solution)/shard_map/ppermute | solution.py:29
  22.2 105.1 %copy-start.40 = (f32[512]{0:T(512)}, f32[512]{0:T(512)S(1)}, u32[]{:S(2)}) copy-start(f32[512]{0:T(512)S(1)} %fusion.107) | copy-start | bytes 6148
  72.5 4.4 collective-permute-start.5
  72.6 6.2 collective-permute-start.4
  78.8 38.0 %collective-permute-start.7 = (bf16[12,4,512]{2,1,0:T(4,128)(2,1)S(1)}, bf16[12,4,512]{2,1,0:T(4,128)(2,1)S(1)}, u32[]{:S(2)}, u32[]{:S(2)}) collective-permute-start(bf16[12,4,512]{2,1,0:T(4,128)(2,1)S(1)} %get-tuple-element.241), channel_id=1, source_target_pairs={{1,0},{2,1},{3,2},{4,3},{5,4},{6,5},{7,6},{0,7},{9,8},{10,9},{11,1... | collective-permute-start | bytes 147464 | tf_op jit(solution)/shard_map/ppermute | solution.py:31
  78.9 37.9 %collective-permute-start.6 = (bf16[12,4,512]{2,1,0:T(4,128)(2,1)S(1)}, bf16[12,4,512]{2,1,0:T(4,128)(2,1)S(1)}, u32[]{:S(2)}, u32[]{:S(2)}) collective-permute-start(bf16[12,4,512]{2,1,0:T(4,128)(2,1)S(1)} %get-tuple-element.240), channel_id=1, source_target_pairs={{0,1},{1,2},{2,3},{3,4},{4,5},{5,6},{6,7},{7,0},{8,9},{9,10},{10,1... | collective-permute-start | bytes 147464 | tf_op jit(solution)/shard_map/ppermute | solution.py:29
  138.9 3.1 collective-permute-start.8
  141.4 4.6 collective-permute-start.9
  141.9 89.2 %all-reduce.11.cloned.1.call-start = ((), (), s32[]{:S(2)}) async-start(), calls=%async_computation.1 | async-start | bytes 262144 | tf_op jit(solution)/shard_map/psum | solution.py:226
  146.8 48.2 %collective-permute-start.11 = (bf16[4,16,512]{2,1,0:T(8,128)(2,1)}, bf16[4,16,512]{2,1,0:T(8,128)(2,1)S(1)}, u32[]{:S(2)}, u32[]{:S(2)}) collective-permute-start(bf16[4,16,512]{2,1,0:T(8,128)(2,1)} %get-tuple-element.239), channel_id=1, source_target_pairs={{0,8},{8,16},{16,24},{1,9},{9,17},{17,25},{2,10},{10,18},{18,26},{... | collective-permute-start | bytes 196616 | tf_op jit(solution)/shard_map/ppermute | solution.py:19
  148.1 46.9 %collective-permute-start.10 = (bf16[4,16,512]{2,1,0:T(8,128)(2,1)}, bf16[4,16,512]{2,1,0:T(8,128)(2,1)S(1)}, u32[]{:S(2)}, u32[]{:S(2)}) collective-permute-start(bf16[4,16,512]{2,1,0:T(8,128)(2,1)} %get-tuple-element.238), channel_id=1, source_target_pairs={{8,0},{16,8},{24,16},{9,1},{17,9},{25,17},{10,2},{18,10},{26,18},{... | collective-permute-start | bytes 196616 | tf_op jit(solution)/shard_map/ppermute | solution.py:19
  152.0 85.8 %copy-start.2 = (f32[512,512]{0,1:T(8,128)}, f32[512,512]{0,1:T(8,128)S(1)}, u32[]{:S(2)}) copy-start(f32[512,512]{0,1:T(8,128)S(1)} %copy.41) | copy-start | bytes 3145732
  194.7 252.6 %all-reduce.13.cloned.1.call-start = ((), (), s32[]{:S(2)}) async-start(), calls=%async_computation.2 | async-start | bytes 29622272 | tf_op jit(solution)/shard_map/psum | solution.py:227
  250.9 700.3 %all-reduce.15.cloned.1.call-start = ((), (), s32[]{:S(2)}) async-start(), calls=%async_computation.3 | async-start | bytes 29622272 | tf_op jit(solution)/shard_map/psum | solution.py:226
  449.7 61.4 %collective-permute-start.12 = (bf16[12,4,512]{2,1,0:T(4,128)(2,1)S(1)}, bf16[12,4,512]{2,1,0:T(4,128)(2,1)S(1)}, u32[]{:S(2)}, u32[]{:S(2)}) collective-permute-start(bf16[12,4,512]{2,1,0:T(4,128)(2,1)S(1)} %get-tuple-element.233), channel_id=1, source_target_pairs={{0,7},{1,0},{2,1},{3,2},{4,3},{5,4},{6,5},{7,6},{8,15},{9,8},{10,9... | collective-permute-start | bytes 147464 | tf_op jit(solution)/shard_map/ppermute | solution.py:13
  451.0 61.7 %collective-permute-start.13 = (bf16[12,4,512]{2,1,0:T(4,128)(2,1)S(1)}, bf16[12,4,512]{2,1,0:T(4,128)(2,1)S(1)}, u32[]{:S(2)}, u32[]{:S(2)}) collective-permute-start(bf16[12,4,512]{2,1,0:T(4,128)(2,1)S(1)} %get-tuple-element.232), channel_id=1, source_target_pairs={{0,1},{1,2},{2,3},{3,4},{4,5},{5,6},{6,7},{7,0},{8,9},{9,10},{10,1... | collective-permute-start | bytes 147464 | tf_op jit(solution)/shard_map/ppermute | solution.py:13
  515.3 4.6 collective-permute-start.15
  516.6 9.4 collective-permute-start.14
  (62 other events, 298.2 us)
Sparse Core Ops, SparseCore 0:
  142.0 52.6 all-reduce.8
  197.0 34.0 all-reduce.10
  251.0 196.2 all-reduce.12
  450.9 500.2 all-reduce.14
